TPU v7x, 256 devices: a whole 4x4x8 slice. The times are simulated.
256 devices in a mesh: section: 2 (over core), srv: 32 (over x, z), tp: 4 (over y).
Axes of the slice: x: 4, y: 4, z: 8, core: 2. Of those that a mesh axis runs over, the one named last changes fastest.
Arguments:
- queries: bfloat16 [8192, 4096], P(('section', 'srv'), 'tp'), may hold values from -40 to 40
- keys: bfloat16 [8192, 512], P(('section', 'srv'), 'tp'), may hold values from -40 to 40
- values: bfloat16 [8192, 512], P(('section', 'srv'), 'tp'), may hold values from -6 to 6
- residual: bfloat16 [8192, 4096], P(('section', 'srv'), 'tp'), may hold values from -6 to 6
- out_weight: bfloat16 [4096, 4096], P('tp', ('section', 'srv')), may hold values from -0.1875 to 0.1875
- norm_gain: float32 [4096], P('tp'), may hold values from 0.25 to 1.75
- level_shift: float32 [8, 4096], P(None, 'tp'), may hold values from -3 to 3
- doc_lengths: int32 [2, 4], P('section'), may hold values from 1 to 128, 256 in all within a row
- noise_level: int32 [2, 4], P('section'), may hold values from 0 to 7
Outputs:
- normed: bfloat16 [8192, 4096], P(('section', 'srv'), 'tp')
Inputs may be any that keep to these rules, and one draw needn't show every extreme that they name: `doc_lengths`: each micro-batch's lengths sum to 256.
All inputs are finite; a program needn't handle non-finite values.
Results may differ from a plain program's by a relative error of at most 0.013.
Values may be sent and summed in bfloat16 or wider, within the bound.
A program may use at most 64 MiB of HBM per device.

v0:
```python
import jax
import jax.numpy as jnp
from jax import lax
from jax.sharding import PartitionSpec as P

D = 4096
HEAD_SIZE = 128
BLK = 16


def in_one_piece(arrays, axis, dim, along):
    ends, at = ([], 0)
    for a in arrays[:-1]:
        at += a.shape[along]
        ends.append(at)
    both = jnp.concatenate(arrays, axis=along)
    return tuple(jnp.split(lax.all_gather(both, axis, axis=dim, tiled=True), ends, axis=along))


def in_blocks(value, dim, length):
    dims = value.shape
    parts = value.reshape(*dims[:dim], length, dims[dim] // length, *dims[dim + 1 :])
    return jnp.moveaxis(parts, dim, 0)


def sent_and_summed(value, axis, dim):
    length = lax.axis_size(axis)
    parts = lax.all_to_all(in_blocks(value, dim, length), axis, 0, 0, tiled=True)
    return jnp.sum(parts.astype(jnp.float32), axis=0)


def from_everyone(value, axis):
    copies = jnp.broadcast_to(value, (lax.axis_size(axis), *value.shape))
    return lax.all_to_all(copies, axis, split_axis=0, concat_axis=0, tiled=True)


def of_everyone(value, axis):
    everything = from_everyone(value, axis)
    return jnp.sum(everything, axis=0)


def bounds(positions, starts, ends):
    member = (positions[:, None] >= starts[None, :]) & (positions[:, None] < ends[None, :])
    first = jnp.sum(jnp.where(member, starts[None, :], 0), axis=1)
    limit = (positions // BLK + 1) * BLK
    return (member, first, limit)


def make_absorb(query_block, first, limit, kv_heads, query_groups):
    rows = query_block.shape[0]
    scale = HEAD_SIZE ** (-0.5)
    grouped = (
        query_block.reshape(rows, kv_heads, query_groups, HEAD_SIZE)
        .transpose(1, 2, 0, 3)
        .reshape(kv_heads, query_groups * rows, HEAD_SIZE)
    )
    row_first = jnp.tile(first, query_groups)
    row_limit = jnp.tile(limit, query_groups)
    empty = (
        jnp.full((kv_heads, query_groups * rows), -1e30, jnp.float32),
        jnp.zeros((kv_heads, query_groups * rows), jnp.float32),
        jnp.zeros((kv_heads, query_groups * rows, HEAD_SIZE), jnp.float32),
    )

    def absorb(carry, pieces, start):
        key_piece, value_piece = pieces
        count = key_piece.shape[0]
        key_pos = jnp.arange(count, dtype=jnp.int32)
        mask = (key_pos[None, :] >= row_first[:, None]) & (key_pos[None, :] < row_limit[:, None])

        def update(state):
            best, total, summed = state
            key_heads = key_piece.reshape(count, kv_heads, HEAD_SIZE)
            value_heads = value_piece.reshape(count, kv_heads, HEAD_SIZE)
            scores = (
                jnp.einsum("kxd,jkd->kxj", grouped, key_heads, preferred_element_type=jnp.float32)
                * scale
            )
            scores = jnp.where(mask[None], scores, -1e30)
            new_best = jnp.maximum(best, jnp.max(scores, axis=-1))
            weights = jnp.where(mask[None], jnp.exp(scores - new_best[..., None]), 0.0)
            total = jnp.sum(weights, axis=-1)
            update_sum = jnp.einsum(
                "kxj,jkd->kxd",
                weights.astype(jnp.bfloat16),
                value_heads,
                preferred_element_type=jnp.float32,
            )
            return (new_best, total, update_sum)

        return lax.cond(jnp.any(mask), update, lambda state: state, carry)

    return (absorb, empty)


def finish(carry, rows, kv_heads, query_groups):
    best, total, summed = carry
    attended = (
        (summed / total[..., None])
        .reshape(kv_heads, query_groups, rows, HEAD_SIZE)
        .transpose(2, 0, 1, 3)
    )
    return attended.reshape(rows, kv_heads * query_groups * HEAD_SIZE).astype(jnp.bfloat16)


def on_device(
    queries, keys, values, residual, out_weight, norm_gain, level_shift, doc_lengths, noise_level
):
    rows = queries.shape[0]
    kv_heads = keys.shape[1] // HEAD_SIZE
    query_groups = queries.shape[1] // keys.shape[1]
    here = lax.axis_index("srv")
    lengths = doc_lengths[0] * BLK
    ends = jnp.cumsum(lengths)
    starts = ends - lengths
    positions = here * rows + jnp.arange(rows, dtype=jnp.int32)
    member, first, limit = bounds(positions, starts, ends)
    absorb, empty = make_absorb(queries, first, limit, kv_heads, query_groups)
    carry = absorb(empty, in_one_piece((keys, values), "srv", 0, 1), jnp.int32(0))
    attended = finish(carry, rows, kv_heads, query_groups)
    partial_sum = jnp.dot(
        attended,
        lax.all_gather(out_weight, ("section", "srv"), axis=1, tiled=True),
        preferred_element_type=jnp.float32,
    )
    share = sent_and_summed(partial_sum.astype(jnp.bfloat16), "tp", 1)
    hidden = residual.astype(jnp.float32) + share
    squares = of_everyone(jnp.sum(hidden * hidden, axis=1), "tp")
    inverse = lax.rsqrt(squares / D + 1e-06)
    level = jnp.sum(jnp.where(member, noise_level[0][None, :], 0), axis=1)
    onehot = (level[:, None] == jnp.arange(level_shift.shape[0], dtype=jnp.int32)[None, :]).astype(
        jnp.float32
    )
    shift = jnp.dot(onehot, level_shift)
    normed = hidden * inverse[:, None] * norm_gain[None, :] * (1.0 + shift)
    return normed.astype(jnp.bfloat16)


def solution(mesh):
    placed = (
        P(("section", "srv"), "tp"),
        P(("section", "srv"), "tp"),
        P(("section", "srv"), "tp"),
        P(("section", "srv"), "tp"),
        P("tp", ("section", "srv")),
        P("tp"),
        P(None, "tp"),
        P("section", None),
        P("section", None),
    )
    return jax.shard_map(
        on_device,
        mesh=mesh,
        in_specs=placed,
        out_specs=P(("section", "srv"), "tp"),
        check_vma=False,
    )
```

profile of v0, /device:TPU:32, one launch (start us, length us, event | category | flops | bytes accessed | tf_op | source)
XLA Modules:
  0.0 215.3 jit_solution(1870984475952749132)
XLA Ops:
  6.5 0.0 copy-start
  6.5 0.0 all-gather.3.cloned.1.call-start
  6.5 1.4 pad_maximum_fusion
  8.0 0.0 all-gather.3.cloned.1.call-update
  8.0 0.0 all-gather.5.cloned.1.call-start
  8.0 0.7 all-gather.5.cloned.1.call-update
  8.7 1.1 copy.23
  9.9 0.7 multiply_bitcast_fusion
  10.5 0.2 reduce-window.4
  10.7 0.7 fusion.18
  11.4 0.7 select_reduce_fusion
  12.1 8.8 %fusion.14 = (pred[1024,4096]{1,0:T(32,128)(4,1)}, pred[]{:T(512)}) fusion(s32[1024]{0:T(1024)S(1)} %broadcast_bitcast_fusion, s32[1024]{0:T(1024)S(1)} %broadcast_bitcast_fusion.1), kind=kLoop, calls=%fused_computation.16 | loop fusion | flops 16777215 | bytes 4202497 | tf_op jit(solution)/shard_map/and | solution.py:69
  21.6 67.9 %all-gather.3.cloned.1.call-done = bf16[4096,256]{1,0:T(8,128)(2,1)} async-done(((bf16[128,256]{1,0:T(8,128)(2,1)}), bf16[4096,256]{1,0:T(8,128)(2,1)}) %all-gather.3.cloned.1.call-update) | async-done | bytes 2097168 | tf_op jit(solution)/shard_map/all_gather | solution.py:17
  89.5 16.3 %conditional.1 = (f32[1,1024]{1,0:T(1,128)S(1)}, f32[1,1024,128]{2,1,0:T(8,128)S(1)}) conditional(s32[]{:T(128)} %convert_element_type.33, () %tuple.13, (bf16[1,8,128,128]{2,3,1,0:T(8,128)(2,1)S(1)}, bf16[4096,256]{1,0:T(8,128)(2,1)}, pred[1024,4096]{1,0:T(32,128)(4,1)}) %tuple.30), branch_computations={%region_3.4_spmd, %region_4.7_spmd} | conditional | flops 2202008576 | bytes 91512904 | solution.py:91
  89.5 0.0 copy-start.3
  89.5 0.2 copy.24
  89.7 0.0 copy-start.1
  89.7 6.0 %fusion = (f32[1024]{0:T(1024)S(1)}, f32[1024,4096]{1,0:T(8,128)S(1)}) fusion(pred[1024,4096]{1,0:T(32,128)(4,1)} %get-tuple-element.15, bf16[1024,128]{1,0:T(8,128)(2,1)S(1)} %bitcast.40, bf16[4096,256]{1,0:T(8,128)(2,1)} %get-tuple-element.17), kind=kOutput, calls=%fused_computation.2 | convolution fusion | flops 1086323712 | bytes 22286336 | tf_op jit(solution)/shard_map/cond/branch_1_fun/kxd,jkd->kxj/dot_general | solution.py:76
  95.7 0.0 copy-done.3
  95.7 0.0 copy-done.1
  95.7 4.3 %fusion.5 = f32[1,1024,128]{2,1,0:T(8,128)S(1)} fusion(pred[1024,4096]{1,0:T(32,128)(4,1)S(1)} %copy-done.1, f32[1024,4096]{1,0:T(8,128)S(1)} %get-tuple-element.40, f32[1024]{0:T(1024)S(1)} %broadcast_maximum_fusion, bf16[4096,256]{1,0:T(8,128)(2,1)S(1)} %copy-done.3), kind=kOutput, calls=%fused_computation.6 | convolution fusion | flops 1094713344 | bytes 22548480 | tf_op jit(solution)/shard_map/cond/branch_1_fun/kxj,jkd->kxd/dot_general | solution.py:83
  100.0 5.6 %fusion.2 = f32[1024]{0:T(1024)S(1)} fusion(pred[1024,4096]{1,0:T(32,128)(4,1)S(1)} %copy-done.1, f32[1024,4096]{1,0:T(8,128)S(1)} %get-tuple-element.40, f32[1024]{0:T(1024)S(1)} %broadcast_maximum_fusion), kind=kLoop, calls=%fused_computation.4 | loop fusion | flops 20970496 | bytes 20979712 | tf_op jit(solution)/shard_map/cond/branch_1_fun/reduce_sum | solution.py:82
  105.8 0.0 copy-start.2
  105.8 0.0 copy-start.4
  105.8 0.2 divide_convert_fusion
  106.0 0.2 copy.25
  106.2 67.3 %all-gather.5.cloned.1.call-done = bf16[1024,4096]{0,1:T(8,128)(2,1)} async-done(((bf16[1024,64]{0,1:T(8,128)(2,1)}), bf16[1024,4096]{0,1:T(8,128)(2,1)}) %all-gather.5.cloned.1.call-update) | async-done | bytes 8388624 | tf_op jit(solution)/shard_map/all_gather | solution.py:123
  173.5 6.3 %convolution_convert_fusion = bf16[128,4096]{1,0:T(8,128)(2,1)S(1)} fusion(bf16[128,1024]{0,1:T(8,128)(2,1)S(1)} %bitcast.41, bf16[1024,4096]{0,1:T(8,128)(2,1)} %all-gather.5.cloned.1.call-done), kind=kOutput, calls=%fused_computation.17 | convolution fusion | flops 1074266112 | bytes 9699328 | tf_op jit(solution)/shard_map/dot_general | solution.py:121
  179.8 0.1 copy.30
  179.9 19.6 %all_to_all.11 = bf16[4,128,1024]{2,1,0:T(8,128)(2,1)S(1)} all-to-all(bf16[4,128,1024]{2,1,0:T(8,128)(2,1)S(1)} %bitcast.39), channel_id=1, replica_groups=mesh['section'=2,'srv'=32,'tp'=4] {'tp'}, dimensions={0} | all-to-all | bytes 2097152 | tf_op jit(solution)/shard_map/all_to_all | solution.py:28
  199.5 0.2 convert_reduce_fusion
  199.7 0.0 copy-done.2
  199.7 0.2 multiply_reduce_fusion
  199.9 7.6 %all_to_all.12 = f32[4,1,128]{2,1,0:T(1,128)S(1)} all-to-all(f32[4,1,128]{2,1,0:T(1,128)S(1)} %broadcast_in_dim.53), channel_id=1, replica_groups=mesh['section'=2,'srv'=32,'tp'=4] {'tp'}, dimensions={0} | all-to-all | bytes 4096 | tf_op jit(solution)/shard_map/all_to_all | solution.py:34
  207.5 0.0 copy-done
  207.5 0.0 copy-done.4
  207.5 1.0 fusion.16
  (7 shorter events, 0.1 us)
Async XLA Ops:
  6.5 201.0 %copy-start = (f32[8,1024]{1,0:T(8,128)S(1)}, f32[8,1024]{1,0:T(8,128)}, u32[]{:S(2)}) copy-start(f32[8,1024]{1,0:T(8,128)} %param.17) | copy-start | bytes 98308
  6.5 83.0 %all-gather.3.cloned.1.call-start = ((), (), s32[]{:S(2)}) async-start(), calls=%async_computation.2 | async-start | bytes 2162688 | tf_op jit(solution)/shard_map/all_gather | solution.py:17
  8.0 165.5 %all-gather.5.cloned.1.call-start = ((), (), s32[]{:S(2)}) async-start(), calls=%async_computation.3 | async-start | bytes 8519680 | tf_op jit(solution)/shard_map/all_gather | solution.py:123
  89.5 6.2 %copy-start.3 = (bf16[4096,256]{1,0:T(8,128)(2,1)S(1)}, bf16[4096,256]{1,0:T(8,128)(2,1)}, u32[]{:S(2)}) copy-start(bf16[4096,256]{1,0:T(8,128)(2,1)} %get-tuple-element.17) | copy-start | bytes 6291460 | tf_op jit(solution)/shard_map/cond
  89.7 6.0 %copy-start.1 = (pred[1024,4096]{1,0:T(32,128)(4,1)S(1)}, pred[1024,4096]{1,0:T(32,128)(4,1)}, u32[]{:S(2)}) copy-start(pred[1024,4096]{1,0:T(32,128)(4,1)} %get-tuple-element.15) | copy-start | bytes 12582916 | tf_op jit(solution)/shard_map/cond
  105.8 93.9 %copy-start.2 = (bf16[128,1024]{1,0:T(8,128)(2,1)S(1)}, bf16[128,1024]{1,0:T(8,128)(2,1)}, u32[]{:S(2)}) copy-start(bf16[128,1024]{1,0:T(8,128)(2,1)} %param.14) | copy-start | bytes 786436
  105.8 101.7 %copy-start.4 = (f32[1024]{0:T(1024)S(1)}, f32[1024]{0:T(1024)}, u32[]{:S(2)}) copy-start(f32[1024]{0:T(1024)} %param.16) | copy-start | bytes 12292
Sparse Core Ops, SparseCore 0:
  10.0 79.5 all-gather.2
  92.3 81.2 all-gather.4
where the time goes:
time: 216 us; the launch traced here: 215 us
  waiting for transfers between devices  136 us (63%)
  blocking collectives  27.2 us (13%)
  other arithmetic  18.6 us (9%)
  matrix products  17.5 us (8%)
  between operations  14.2 us (7%)
    all_gather x1, waiting for transfers between devices, in_one_piece(): lax.all_gather(both, axis, axis=dim, tiled=True)  67.9 us
    all_gather x1, waiting for transfers between devices, on_device(): lax.all_gather(out_weight, ('section', 'srv'), axis=1, tiled=True)  67.3 us
    all_to_all x1, blocking collectives, sent_and_summed(): lax.all_to_all(in_blocks(value, dim, length), axis, 0, 0, tiled=True)  19.6 us
    and x1, other arithmetic, absorb(): (key_pos[None, :] >= row_first[:, None]) & (key_pos[None, :] < row_limit[...  8.79 us
    all_to_all x1, blocking collectives, from_everyone(): return lax.all_to_all(copies, axis, split_axis=0, concat_axis=0, tiled=True)  7.59 us
    dot_general x1, matrix products, on_device(): jnp.dot(attended, lax.all_gather(out_weight, ('section', 'srv'), axis=1,...  6.28 us
    dot_general x1, matrix products, update(): jnp.einsum('kxd,jkd->kxj', grouped, key_heads, preferred_element_type=jnp...  5.97 us
    reduce_sum x1, other arithmetic, update(): total = jnp.sum(weights, axis=-1)  5.58 us
  transfers between devices with their start and end apart: 2, of which 2 were waited for; matrix products, arithmetic and copies ran while one was open for 13% of the time, Pallas kernels for 0%

commit v1 on v0

--- a/solution.py
+++ b/solution.py
@@ -120,7 +120,15 @@
     attended = finish(carry, rows, kv_heads, query_groups)
     partial_sum = jnp.dot(
         attended,
-        lax.all_gather(out_weight, ("section", "srv"), axis=1, tiled=True),
+        jnp.concatenate(
+            lax.all_to_all(
+                jnp.stack([out_weight] * lax.axis_size(("section", "srv"))),
+                ("section", "srv"),
+                0,
+                0,
+            ),
+            axis=1,
+        ),
         preferred_element_type=jnp.float32,
     )
     share = sent_and_summed(partial_sum.astype(jnp.bfloat16), "tp", 1)

time: 216 us -> 269 us (1.25)
  waiting for transfers between devices: 136 us -> 175 us
  starting transfers between devices: 0.04 us -> 12 us
  local copies, waits for them, and re-layouts: 1.6 us -> 5.86 us
  other arithmetic: 18.6 us -> 15.8 us
    all_gather x1 -> x0, waiting for transfers between devices: 67.3 us -> none  [on_device(): lax.all_gather(out_weight, ('section', 'srv'), axis=1, tiled=True)]
    all_to_all x0 -> x1, waiting for transfers between devices: none -> 59.1 us  [on_device(): lax.all_to_all(jnp.stack([out_weight] * lax.axis_size(('section', 'srv'))...]
    all_gather x1, waiting for transfers between devices: 67.9 us -> 116 us  [in_one_piece(): lax.all_gather(both, axis, axis=dim, tiled=True)]
    all_to_all x0 -> x1, starting transfers between devices: none -> 11.9 us  [on_device(): lax.all_to_all(jnp.stack([out_weight] * lax.axis_size(('section', 'srv'))...]
    another operation x1 -> x2, local copies, waits for them, and re-layouts: 0.18 us -> 5.37 us  [the longest x1 5.19 us: on_device(): jnp.stack([out_weight] * lax.axis_size(('section', 'srv')))]
  transfers between devices with their start and end apart: 2 -> 2, of which waited for: 2 -> 2; matrix products, arithmetic and copies ran while one was open for 13% -> 10% of each run, Pallas kernels for 0% -> 0%
where the time goes in v1:
time: 269 us; the launch traced here: 267 us
  waiting for transfers between devices  175 us (65%)
  blocking collectives  27.1 us (10%)
  matrix products  17.5 us (7%)
  other arithmetic  15.8 us (6%)
  between operations  14.2 us (5%)
  starting transfers between devices  12 us (4%)
  local copies, waits for them, and re-layouts  5.86 us (2%)
    all_gather x1, waiting for transfers between devices, in_one_piece(): lax.all_gather(both, axis, axis=dim, tiled=True)  116 us
    all_to_all x1, waiting for transfers between devices, on_device(): lax.all_to_all(jnp.stack([out_weight] * lax.axis_size(('section', 'srv'))...  59.1 us
    all_to_all x1, blocking collectives, sent_and_summed(): lax.all_to_all(in_blocks(value, dim, length), axis, 0, 0, tiled=True)  19.5 us
    all_to_all x1, starting transfers between devices, on_device(): lax.all_to_all(jnp.stack([out_weight] * lax.axis_size(('section', 'srv'))...  11.9 us
    and x1, other arithmetic, absorb(): (key_pos[None, :] >= row_first[:, None]) & (key_pos[None, :] < row_limit[...  8.72 us
    all_to_all x1, blocking collectives, from_everyone(): return lax.all_to_all(copies, axis, split_axis=0, concat_axis=0, tiled=True)  7.59 us
    dot_general x1, matrix products, on_device(): jnp.dot(attended, jnp.concatenate(lax.all_to_all(jnp.stack([out_weight] *...  6.28 us
    dot_general x1, matrix products, update(): jnp.einsum('kxd,jkd->kxj', grouped, key_heads, preferred_element_type=jnp...  5.97 us
  transfers between devices with their start and end apart: 2, of which 2 were waited for; matrix products, arithmetic and copies ran while one was open for 10% of the time, Pallas kernels for 0%

profile of v1, /device:TPU:32, one launch (start us, length us, event | category | flops | bytes accessed | tf_op | source)
XLA Modules:
  0.0 267.3 jit_solution(13706088003604370948)
XLA Ops:
  6.5 0.0 copy-start
  6.5 5.2 %stack.2 = bf16[64,1024,64]{1,2,0:T(8,128)(2,1)} broadcast(bf16[1024,64]{0,1:T(8,128)(2,1)} %param.15), dimensions={1,2} | broadcast | bytes 8519680 | tf_op jit(solution)/shard_map/stack | solution.py:125
  11.7 0.0 copy-start.5
  11.7 0.0 copy-start.6
  11.7 0.0 copy-start.4
  11.7 0.0 copy-start.9
  11.7 0.0 copy-start.8
  11.8 11.9 %all-to-all-start = ((bf16[64,1024,64]{1,2,0:T(8,128)(2,1)}), bf16[64,1024,64]{1,2,0:T(8,128)(2,1)}, u32[]{:S(2)}, u32[]{:S(2)}) async-start(bf16[64,1024,64]{1,2,0:T(8,128)(2,1)} %stack.2), calls=%async_computation | async-start | bytes 16777216 | tf_op jit(solution)/shard_map/all_to_all | solution.py:124
  23.7 0.0 all-gather.2.cloned.1.call-start
  23.7 0.0 copy-done.5
  23.7 0.0 copy-done.6
  23.8 0.6 pad_maximum_fusion
  24.4 0.0 all-gather.2.cloned.1.call-update
  24.4 0.0 copy-done.4
  24.4 0.2 copy.24
  24.6 0.0 copy-done.9
  24.6 0.2 reduce-window.4
  24.8 0.0 copy-done.8
  24.8 0.1 select_reduce_fusion
  24.9 8.7 %fusion.14 = (pred[1024,4096]{1,0:T(32,128)(4,1)}, pred[]{:T(512)}) fusion(s32[1024]{0:T(1024)S(1)} %broadcast_bitcast_fusion, s32[1024]{0:T(1024)S(1)} %broadcast_bitcast_fusion.1), kind=kLoop, calls=%fused_computation.16 | loop fusion | flops 16777215 | bytes 4202497 | tf_op jit(solution)/shard_map/and | solution.py:69
  34.2 115.5 %all-gather.2.cloned.1.call-done = bf16[4096,256]{1,0:T(8,128)(2,1)} async-done(((bf16[128,256]{1,0:T(8,128)(2,1)}), bf16[4096,256]{1,0:T(8,128)(2,1)}) %all-gather.2.cloned.1.call-update) | async-done | bytes 2097168 | tf_op jit(solution)/shard_map/all_gather | solution.py:17
  149.7 16.3 %conditional.1 = (f32[1,1024]{1,0:T(1,128)S(1)}, f32[1,1024,128]{2,1,0:T(8,128)S(1)}) conditional(s32[]{:T(128)} %convert_element_type.33, () %tuple.13, (bf16[1,8,128,128]{2,3,1,0:T(8,128)(2,1)S(1)}, bf16[4096,256]{1,0:T(8,128)(2,1)}, pred[1024,4096]{1,0:T(32,128)(4,1)}) %tuple.28), branch_computations={%region_3.4_spmd, %region_4.7_spmd} | conditional | flops 2202008576 | bytes 91512904 | solution.py:91
  149.7 0.2 copy.25
  149.9 0.0 copy-start.1
  149.9 0.0 copy-start.3
  150.0 6.0 %fusion = (f32[1024]{0:T(1024)S(1)}, f32[1024,4096]{1,0:T(8,128)S(1)}) fusion(pred[1024,4096]{1,0:T(32,128)(4,1)} %get-tuple-element.15, bf16[1024,128]{1,0:T(8,128)(2,1)S(1)} %bitcast.43, bf16[4096,256]{1,0:T(8,128)(2,1)} %get-tuple-element.17), kind=kOutput, calls=%fused_computation.2 | convolution fusion | flops 1086323712 | bytes 22286336 | tf_op jit(solution)/shard_map/cond/branch_1_fun/kxd,jkd->kxj/dot_general | solution.py:76
  155.9 0.0 copy-done.1
  156.0 0.0 copy-done.3
  156.0 4.3 %fusion.5 = f32[1,1024,128]{2,1,0:T(8,128)S(1)} fusion(pred[1024,4096]{1,0:T(32,128)(4,1)S(1)} %copy-done.1, f32[1024,4096]{1,0:T(8,128)S(1)} %get-tuple-element.40, f32[1024]{0:T(1024)S(1)} %broadcast_maximum_fusion, bf16[4096,256]{1,0:T(8,128)(2,1)S(1)} %copy-done.3), kind=kOutput, calls=%fused_computation.6 | convolution fusion | flops 1094713344 | bytes 22548480 | tf_op jit(solution)/shard_map/cond/branch_1_fun/kxj,jkd->kxd/dot_general | solution.py:83
  160.3 5.6 %fusion.2 = f32[1024]{0:T(1024)S(1)} fusion(pred[1024,4096]{1,0:T(32,128)(4,1)S(1)} %copy-done.1, f32[1024,4096]{1,0:T(8,128)S(1)} %get-tuple-element.40, f32[1024]{0:T(1024)S(1)} %broadcast_maximum_fusion), kind=kLoop, calls=%fused_computation.4 | loop fusion | flops 20970496 | bytes 20979712 | tf_op jit(solution)/shard_map/cond/branch_1_fun/reduce_sum | solution.py:82
  166.0 0.0 copy-start.2
  166.0 0.2 divide_convert_fusion
  166.3 0.0 copy-start.7
  166.3 0.2 copy.26
  166.5 59.1 %all-to-all-done = bf16[64,1024,64]{1,2,0:T(8,128)(2,1)} async-done(((bf16[64,1024,64]{1,2,0:T(8,128)(2,1)}), bf16[64,1024,64]{1,2,0:T(8,128)(2,1)}, u32[]{:S(2)}, u32[]{:S(2)}) %all-to-all-start) | async-done | bytes 8388640 | tf_op jit(solution)/shard_map/all_to_all | solution.py:124
  225.6 6.3 %convolution_convert_fusion = bf16[128,4096]{1,0:T(8,128)(2,1)S(1)} fusion(bf16[128,1024]{0,1:T(8,128)(2,1)S(1)} %bitcast.44, bf16[1024,4096]{0,1:T(8,128)(2,1)} %bitcast.16), kind=kOutput, calls=%fused_computation.17 | convolution fusion | flops 1074266112 | bytes 9699328 | tf_op jit(solution)/shard_map/dot_general | solution.py:121
  231.8 0.1 copy.31
  231.9 19.5 %all_to_all.16 = bf16[4,128,1024]{2,1,0:T(8,128)(2,1)S(1)} all-to-all(bf16[4,128,1024]{2,1,0:T(8,128)(2,1)S(1)} %bitcast.42), channel_id=1, replica_groups=mesh['section'=2,'srv'=32,'tp'=4] {'tp'}, dimensions={0} | all-to-all | bytes 2097152 | tf_op jit(solution)/shard_map/all_to_all | solution.py:28
  251.5 0.2 convert_reduce_fusion
  251.7 0.0 copy-done.2
  251.7 0.2 multiply_reduce_fusion
  251.8 7.6 %all_to_all.17 = f32[4,1,128]{2,1,0:T(1,128)S(1)} all-to-all(f32[4,1,128]{2,1,0:T(1,128)S(1)} %broadcast_in_dim.53), channel_id=1, replica_groups=mesh['section'=2,'srv'=32,'tp'=4] {'tp'}, dimensions={0} | all-to-all | bytes 4096 | tf_op jit(solution)/shard_map/all_to_all | solution.py:34
  259.5 0.0 copy-done
  259.5 0.0 copy-done.7
  259.5 1.0 fusion.16
  (9 shorter events, 0.1 us)
Async XLA Ops:
  6.5 252.9 %copy-start = (f32[8,1024]{1,0:T(8,128)S(1)}, f32[8,1024]{1,0:T(8,128)}, u32[]{:S(2)}) copy-start(f32[8,1024]{1,0:T(8,128)} %param.17) | copy-start | bytes 98308
  11.7 12.0 %copy-start.5 = (bf16[128,128]{1,0:T(8,128)(2,1)S(1)}, bf16[128,128]{1,0:T(8,128)(2,1)}, u32[]{:S(2)}) copy-start(bf16[128,128]{1,0:T(8,128)(2,1)} %param.13) | copy-start | bytes 98308
  11.7 12.0 %copy-start.6 = (bf16[128,128]{1,0:T(8,128)(2,1)S(1)}, bf16[128,128]{1,0:T(8,128)(2,1)}, u32[]{:S(2)}) copy-start(bf16[128,128]{1,0:T(8,128)(2,1)} %param.12) | copy-start | bytes 98308
  11.7 12.7 %copy-start.4 = (bf16[128,1024]{1,0:T(8,128)(2,1)S(1)}, bf16[128,1024]{1,0:T(8,128)(2,1)}, u32[]{:S(2)}) copy-start(bf16[128,1024]{1,0:T(8,128)(2,1)} %param.11) | copy-start | bytes 786436
  11.7 12.9 %copy-start.9 = (s32[1,4]{1,0:T(1,128)S(1)}, s32[1,4]{1,0:T(1,128)}, u32[]{:S(2)}) copy-start(s32[1,4]{1,0:T(1,128)} %param.18) | copy-start | bytes 52
  11.7 13.1 %copy-start.8 = (s32[1,4]{1,0:T(1,128)S(1)}, s32[1,4]{1,0:T(1,128)}, u32[]{:S(2)}) copy-start(s32[1,4]{1,0:T(1,128)} %param.19) | copy-start | bytes 52
  11.8 213.8 %all-to-all-start = ((bf16[64,1024,64]{1,2,0:T(8,128)(2,1)}), bf16[64,1024,64]{1,2,0:T(8,128)(2,1)}, u32[]{:S(2)}, u32[]{:S(2)}) async-start(bf16[64,1024,64]{1,2,0:T(8,128)(2,1)} %stack.2), calls=%async_computation | async-start | bytes 16777216 | tf_op jit(solution)/shard_map/all_to_all | solution.py:124
  23.7 126.1 %all-gather.2.cloned.1.call-start = ((), (), s32[]{:S(2)}) async-start(), calls=%async_computation.3 | async-start | bytes 2162688 | tf_op jit(solution)/shard_map/all_gather | solution.py:17
  149.9 6.0 %copy-start.1 = (pred[1024,4096]{1,0:T(32,128)(4,1)S(1)}, pred[1024,4096]{1,0:T(32,128)(4,1)}, u32[]{:S(2)}) copy-start(pred[1024,4096]{1,0:T(32,128)(4,1)} %get-tuple-element.15) | copy-start | bytes 12582916 | tf_op jit(solution)/shard_map/cond
  149.9 6.0 %copy-start.3 = (bf16[4096,256]{1,0:T(8,128)(2,1)S(1)}, bf16[4096,256]{1,0:T(8,128)(2,1)}, u32[]{:S(2)}) copy-start(bf16[4096,256]{1,0:T(8,128)(2,1)} %get-tuple-element.17) | copy-start | bytes 6291460 | tf_op jit(solution)/shard_map/cond
  166.0 85.6 %copy-start.2 = (bf16[128,1024]{1,0:T(8,128)(2,1)S(1)}, bf16[128,1024]{1,0:T(8,128)(2,1)}, u32[]{:S(2)}) copy-start(bf16[128,1024]{1,0:T(8,128)(2,1)} %param.14) | copy-start | bytes 786436
  166.3 93.2 %copy-start.7 = (f32[1024]{0:T(1024)S(1)}, f32[1024]{0:T(1024)}, u32[]{:S(2)}) copy-start(f32[1024]{0:T(1024)} %param.16) | copy-start | bytes 12292
Sparse Core Ops, SparseCore 0:
  27.1 122.5 all-gather.1
